TPU v7x, 32 devices: a whole 2x2x4 slice. The times are simulated.
32 devices in a mesh: gx: 4 (over z), gy: 8 (over y, x, core).
Axes of the slice: x: 2, y: 2, z: 4, core: 2. Of those that a mesh axis runs over, the one named last changes fastest.
Arguments:
- centres: bfloat16 [131072, 256], P(('gx', 'gy')), may hold values from -20 to 20
- weights: float32 [16, 131072], P(None, ('gx', 'gy')), may hold values from -1 to 1
- targets: float32 [16, 256], P(None, ('gx', 'gy')), may hold values from -6 to 6
- batch_index: int32 [256], P(('gx', 'gy')), may hold values from 0 to 131071, as said below
- nystrom_index: int32 [2048], P(('gx', 'gy')), may hold values from 0 to 131071, as said below
- eigvecs: float32 [2048, 128], P(('gx', 'gy')), may hold values from -0.125 to 0.125
- scales: float32 [128], replicated, may hold values from 0.2 to 2
Outputs:
- residual: float32 [16, 256], P(None, ('gx', 'gy'))
- block_correction: float32 [16, 2048], P(None, ('gx', 'gy'))
Inputs may be any that keep to these rules, and one draw needn't show every extreme that they name: `batch_index`: the entries at positions j * 8 to (j + 1) * 8 - 1 name centres j * 4096 to (j + 1) * 4096 - 1, all different. `nystrom_index`: the entries at positions j * 64 to (j + 1) * 64 - 1 name centres j * 4096 to (j + 1) * 4096 - 1, all different.
All inputs are finite; a program needn't handle non-finite values.
Results may differ from a plain program's by a relative error of at most 0.0003.
Values may be sent and summed in bfloat16 or wider, within the bound.
A program may use at most 192 MiB of HBM per device.

v0:
```python
import jax
import jax.numpy as jnp
from jax import lax
from jax.sharding import PartitionSpec as P


def kernel_tile(points, point_norm, others, other_norm):
    width = float(points.shape[1]) ** 0.5
    inner = jnp.dot(points, others.T, preferred_element_type=jnp.float32)
    squared = point_norm[:, None] + other_norm[None, :] - 2.0 * inner
    return jnp.exp(-jnp.sqrt(jnp.maximum(squared, 1.0)) / width)


def combine_projection(partial_projection):
    return lax.psum(partial_projection, ("gx", "gy"))


def on_device(centres, weights, targets, batch_index, nystrom_index, eigvecs, scales):
    device_rank = lax.axis_index(("gx", "gy"))
    local_count = centres.shape[0]
    outputs = weights.shape[0]
    local_batch = batch_index - device_rank * local_count
    local_block = nystrom_index - device_rank * local_count
    batch_local = jnp.take(centres, local_batch, axis=0)
    centre_norm = jnp.sum(centres.astype(jnp.float32) ** 2, axis=1)
    rows_in = lax.all_gather(batch_local, ("gx", "gy"), axis=0, tiled=True)
    rows_norm = jnp.sum(rows_in.astype(jnp.float32) ** 2, axis=1)
    tile = kernel_tile(rows_in, rows_norm, centres, centre_norm)
    predicted = lax.dot_general(
        weights, tile, (((1,), (1,)), ((), ())), precision=lax.Precision.HIGHEST
    )
    block_tile = jnp.take(tile, local_block, axis=1)
    carried = block_tile.T
    gathered = jnp.concatenate([predicted, carried], axis=0)
    partial_prediction = gathered[:outputs]
    carried = gathered[outputs:]
    inner_sum = lax.psum(partial_prediction, "gy")
    reduced = lax.psum(inner_sum, "gx")
    targets_full = lax.all_gather(targets, ("gx", "gy"), axis=1, tiled=True)
    residual_full = reduced - targets_full
    residual_local = lax.dynamic_slice_in_dim(
        residual_full, device_rank * batch_local.shape[0], batch_local.shape[0], 1
    )
    along = jnp.dot(carried, residual_full.T, precision=lax.Precision.HIGHEST)
    projection = combine_projection(jnp.dot(eigvecs.T, along, precision=lax.Precision.HIGHEST))
    correction = jnp.dot(eigvecs * scales[None, :], projection, precision=lax.Precision.HIGHEST)
    return (residual_local, correction.T)


def solution(mesh):
    return jax.shard_map(
        on_device,
        mesh=mesh,
        in_specs=(
            P(("gx", "gy"), None),
            P(None, ("gx", "gy")),
            P(None, ("gx", "gy")),
            P(("gx", "gy")),
            P(("gx", "gy")),
            P(("gx", "gy"), None),
            P(),
        ),
        out_specs=(P(None, ("gx", "gy")), P(None, ("gx", "gy"))),
        check_vma=False,
    )
```

profile of v0, /device:TPU:14, one launch (start us, length us, event | category | flops | bytes accessed | tf_op | source)
XLA Modules:
  0.0 182.1 jit_solution(13803542961892802203)
XLA Ops:
  0.6 0.0 copy-start
  0.7 0.7 compare_and_fusion.1
  1.4 2.4 %gather_fusion = bf16[8,256]{1,0:T(8,128)(2,1)S(1)} fusion(bf16[4096,256]{1,0:T(8,128)(2,1)} %param.7, s32[1024]{0:T(1024)S(1)} %pad_clamp_fusion.1), kind=kCustom, calls=%fused_computation | custom fusion | bytes 8224 | tf_op jit(solution)/shard_map/jit(_take)/gather | solution.py:24
  3.8 0.1 broadcast_select_fusion
  3.9 29.1 %all_gather.6 = bf16[256,256]{1,0:T(8,128)(2,1)S(1)} all-gather(bf16[8,256]{1,0:T(8,128)(2,1)S(1)} %broadcast_select_fusion), channel_id=1, replica_groups=mesh['gx'=4,'gy'=8] {'gx','gy'}, dimensions={0}, use_global_device_ids=true | all-gather | bytes 135168 | tf_op jit(solution)/shard_map/all_gather | solution.py:26
  33.0 2.2 %multiply_reduce_fusion = f32[4096]{0:T(1024)S(1)} fusion(bf16[4096,256]{1,0:T(8,128)(2,1)} %param.7), kind=kLoop, calls=%fused_computation.9 | loop fusion | flops 3141632 | bytes 2113536 | tf_op jit(solution)/shard_map/reduce_sum | solution.py:25
  35.2 0.1 multiply_reduce_fusion.1
  35.3 3.8 %fusion.5 = f32[256,4096]{1,0:T(8,128)S(1)} fusion(bf16[256,256]{1,0:T(8,128)(2,1)S(1)} %all_gather.6, bf16[4096,256]{1,0:T(8,128)(2,1)} %param.7, f32[4096]{0:T(1024)S(1)} %multiply_reduce_fusion, f32[256]{0:T(256)S(1)} %multiply_reduce_fusion.1), kind=kOutput, calls=%fused_computation.8 | convolution fusion | flops 543162368 | bytes 6439936 | tf_op jit(solution)/shard_map/dot_general | solution.py:9
  39.2 0.0 copy-start.1
  39.2 1.9 %copy-done.1 = f32[256,4096]{1,0:T(8,128)} copy-done((f32[256,4096]{1,0:T(8,128)}, f32[256,4096]{1,0:T(8,128)S(1)}, u32[]{:S(2)}) %copy-start.1) | copy-done | bytes 4194328
  41.1 0.0 copy-done
  41.1 0.0 copy-start.3
  41.1 3.3 %convolution_bitcast_fusion = f32[16,256]{1,0:T(8,128)S(1)} fusion(f32[256,4096]{1,0:T(8,128)S(1)} %fusion.5, f32[16,4096]{1,0:T(8,128)S(1)} %copy-done), kind=kOutput, calls=%fused_computation.10 | convolution fusion | flops 201326592 | bytes 4472832 | tf_op jit(solution)/shard_map/dot_general | solution.py:29
  44.4 25.5 %psum.21 = f32[16,256]{1,0:T(8,128)S(1)} all-reduce(f32[16,256]{1,0:T(8,128)S(1)} %convolution_bitcast_fusion), channel_id=1, replica_groups=mesh['gx'=4,'gy'=8] {'gy'}, use_global_device_ids=true, to_apply=%region_2.3 | all-reduce | flops 4096 | bytes 32768 | tf_op jit(solution)/shard_map/psum | solution.py:37
  70.0 20.5 %psum.22 = f32[16,256]{1,0:T(8,128)S(1)} all-reduce(f32[16,256]{1,0:T(8,128)S(1)} %psum.21), channel_id=1, replica_groups=mesh['gx'=4,'gy'=8] {'gx'}, use_global_device_ids=true, to_apply=%region_3.4 | all-reduce | flops 4096 | bytes 32768 | tf_op jit(solution)/shard_map/psum | solution.py:38
  90.5 0.0 copy-done.3
  90.5 32.1 %all_gather.7 = f32[16,256]{0,1:T(8,128)S(1)} all-gather(f32[16,8]{0,1:T(8,128)S(1)} %copy-done.3), channel_id=1, replica_groups=mesh['gx'=4,'gy'=8] {'gx','gy'}, dimensions={1}, use_global_device_ids=true | all-gather | bytes 16896 | tf_op jit(solution)/shard_map/all_gather | solution.py:39
  122.5 0.1 copy.12
  122.6 0.1 constant_dynamic-slice_fusion
  122.7 0.7 copy.14
  123.4 0.0 copy-start.5
  123.4 0.0 copy-start.2
  123.4 0.0 copy-start.4
  123.4 5.6 %copy.13 = f32[256,4096]{0,1:T(8,128)} copy(f32[256,4096]{1,0:T(8,128)} %copy-done.1) | data formatting | bytes 8388608 | tf_op jit(solution)/shard_map/exp | solution.py:11
  129.0 0.0 copy-done.5
  129.0 2.8 %gather_fusion.1 = f32[64,256]{1,0:T(8,128)S(1)} fusion(f32[256,4096]{0,1:T(8,128)} %copy.13, s32[1024]{0:T(1024)S(1)} %pad_clamp_fusion), kind=kCustom, calls=%fused_computation.1 | custom fusion | bytes 131328 | tf_op jit(solution)/shard_map/jit(_take)/gather | solution.py:32
  131.9 0.3 fusion.6
  132.1 0.0 copy-done.2
  132.2 0.2 convolution_bitcast_fusion.1
  132.4 49.0 %psum.23 = f32[128,16]{0,1:T(8,128)S(1)} all-reduce(f32[128,16]{0,1:T(8,128)S(1)} %convolution_bitcast_fusion.1), channel_id=1, replica_groups=mesh['gx'=4,'gy'=8] {'gx','gy'}, use_global_device_ids=true, to_apply=%region_4.5 | all-reduce | flops 2048 | bytes 16384 | tf_op jit(solution)/shard_map/psum | solution.py:15
  181.3 0.0 copy-done.4
  181.3 0.8 fusion.9
  (4 shorter events, 0.0 us)
Async XLA Ops:
  0.6 40.5 %copy-start = (f32[16,4096]{1,0:T(8,128)S(1)}, f32[16,4096]{1,0:T(8,128)}, u32[]{:S(2)}) copy-start(f32[16,4096]{1,0:T(8,128)} %param.8) | copy-start | bytes 786436
  39.2 1.9 %copy-start.1 = (f32[256,4096]{1,0:T(8,128)}, f32[256,4096]{1,0:T(8,128)S(1)}, u32[]{:S(2)}) copy-start(f32[256,4096]{1,0:T(8,128)S(1)} %fusion.5) | copy-start | bytes 12582916
  41.1 49.4 %copy-start.3 = (f32[16,8]{0,1:T(8,128)S(1)}, f32[16,8]{0,1:T(8,128)}, u32[]{:S(2)}) copy-start(f32[16,8]{0,1:T(8,128)} %param.9) | copy-start | bytes 1540
  123.4 5.6 %copy-start.5 = (s32[64]{0:T(128)S(1)}, s32[64]{0:T(128)}, u32[]{:S(2)}) copy-start(s32[64]{0:T(128)} %param.11) | copy-start | bytes 772
  123.4 8.8 %copy-start.2 = (f32[64,128]{1,0:T(8,128)S(1)}, f32[64,128]{1,0:T(8,128)}, u32[]{:S(2)}) copy-start(f32[64,128]{1,0:T(8,128)} %param.12) | copy-start | bytes 98308
  123.4 58.0 %copy-start.4 = (f32[128]{0:T(128)S(1)}, f32[128]{0:T(128)}, u32[]{:S(2)}) copy-start(f32[128]{0:T(128)} %param.13) | copy-start | bytes 1540
where the time goes:
time: 183 us; the launch traced here: 182 us
  blocking collectives  156 us (85%)
  local copies, waits for them, and re-layouts  13.7 us (7%)
  matrix products  8.4 us (5%)
  other arithmetic  3.13 us (2%)
    psum x1, blocking collectives, combine_projection(): return lax.psum(partial_projection, ('gx', 'gy'))  49 us
    all_gather x1, blocking collectives, on_device(): targets_full = lax.all_gather(targets, ('gx', 'gy'), axis=1, tiled=True)  32.1 us
    all_gather x1, blocking collectives, on_device(): rows_in = lax.all_gather(batch_local, ('gx', 'gy'), axis=0, tiled=True)  29.1 us
    psum x1, blocking collectives, on_device(): inner_sum = lax.psum(partial_prediction, 'gy')  25.5 us
    psum x1, blocking collectives, on_device(): reduced = lax.psum(inner_sum, 'gx')  20.5 us
    exp x1, local copies, waits for them, and re-layouts, kernel_tile(): return jnp.exp(-jnp.sqrt(jnp.maximum(squared, 1.0)) / width)  5.64 us
    dot_general x1, matrix products, kernel_tile(): inner = jnp.dot(points, others.T, preferred_element_type=jnp.float32)  3.82 us

commit v1 on v0

--- a/solution.py
+++ b/solution.py
@@ -2,6 +2,12 @@
 import jax.numpy as jnp
 from jax import lax
 from jax.sharding import PartitionSpec as P
+
+
+def add_all(x, mesh_axis):
+    blocks = lax.all_gather(x, mesh_axis, axis=0, tiled=False)
+    total = blocks.sum(axis=0)
+    return total
 
 
 def kernel_tile(points, point_norm, others, other_norm):
@@ -34,7 +40,7 @@
     gathered = jnp.concatenate([predicted, carried], axis=0)
     partial_prediction = gathered[:outputs]
     carried = gathered[outputs:]
-    inner_sum = lax.psum(partial_prediction, "gy")
+    inner_sum = add_all(partial_prediction, "gy")
     reduced = lax.psum(inner_sum, "gx")
     targets_full = lax.all_gather(targets, ("gx", "gy"), axis=1, tiled=True)
     residual_full = reduced - targets_full

time: 183 us -> 169 us (0.923)
  blocking collectives: 156 us -> 142 us
    psum x1 -> x0, blocking collectives: 25.5 us -> none  [on_device(): inner_sum = lax.psum(partial_prediction, 'gy')]
    all_gather x0 -> x1, blocking collectives: none -> 13.6 us  [add_all(): blocks = lax.all_gather(x, mesh_axis, axis=0, tiled=False)]
    all_gather x1, blocking collectives: 32.1 us -> 29.9 us  [on_device(): targets_full = lax.all_gather(targets, ('gx', 'gy'), axis=1, tiled=True)]
where the time goes in v1:
time: 169 us; the launch traced here: 168 us
  blocking collectives  142 us (84%)
  local copies, waits for them, and re-layouts  13.7 us (8%)
  matrix products  8.3 us (5%)
  other arithmetic  3.14 us (2%)
    psum x1, blocking collectives, combine_projection(): return lax.psum(partial_projection, ('gx', 'gy'))  48.8 us
    all_gather x1, blocking collectives, on_device(): targets_full = lax.all_gather(targets, ('gx', 'gy'), axis=1, tiled=True)  29.9 us
    all_gather x1, blocking collectives, on_device(): rows_in = lax.all_gather(batch_local, ('gx', 'gy'), axis=0, tiled=True)  29.1 us
    psum x1, blocking collectives, on_device(): reduced = lax.psum(inner_sum, 'gx')  20.4 us
    all_gather x1, blocking collectives, add_all(): blocks = lax.all_gather(x, mesh_axis, axis=0, tiled=False)  13.6 us
    exp x1, local copies, waits for them, and re-layouts, kernel_tile(): return jnp.exp(-jnp.sqrt(jnp.maximum(squared, 1.0)) / width)  5.64 us
    dot_general x1, matrix products, kernel_tile(): inner = jnp.dot(points, others.T, preferred_element_type=jnp.float32)  3.82 us

profile of v1, /device:TPU:14, one launch (start us, length us, event | category | flops | bytes accessed | tf_op | source)
XLA Modules:
  0.0 167.7 jit_solution(16811128615719097566)
XLA Ops:
  0.6 0.0 copy-start
  0.7 0.7 compare_and_fusion.1
  1.4 2.4 %gather_fusion = bf16[8,256]{1,0:T(8,128)(2,1)S(1)} fusion(bf16[4096,256]{1,0:T(8,128)(2,1)} %param.7, s32[1024]{0:T(1024)S(1)} %pad_clamp_fusion.1), kind=kCustom, calls=%fused_computation | custom fusion | bytes 8224 | tf_op jit(solution)/shard_map/jit(_take)/gather | solution.py:30
  3.8 0.1 broadcast_select_fusion
  3.9 29.1 %all_gather.12 = bf16[256,256]{1,0:T(8,128)(2,1)S(1)} all-gather(bf16[8,256]{1,0:T(8,128)(2,1)S(1)} %broadcast_select_fusion), channel_id=1, replica_groups=mesh['gx'=4,'gy'=8] {'gx','gy'}, dimensions={0}, use_global_device_ids=true | all-gather | bytes 135168 | tf_op jit(solution)/shard_map/all_gather | solution.py:32
  33.0 2.2 %multiply_reduce_fusion = f32[4096]{0:T(1024)S(1)} fusion(bf16[4096,256]{1,0:T(8,128)(2,1)} %param.7), kind=kLoop, calls=%fused_computation.9 | loop fusion | flops 3141632 | bytes 2113536 | tf_op jit(solution)/shard_map/reduce_sum | solution.py:31
  35.2 0.1 multiply_reduce_fusion.1
  35.3 3.8 %fusion.5 = f32[256,4096]{1,0:T(8,128)S(1)} fusion(bf16[256,256]{1,0:T(8,128)(2,1)S(1)} %all_gather.12, bf16[4096,256]{1,0:T(8,128)(2,1)} %param.7, f32[4096]{0:T(1024)S(1)} %multiply_reduce_fusion, f32[256]{0:T(256)S(1)} %multiply_reduce_fusion.1), kind=kOutput, calls=%fused_computation.8 | convolution fusion | flops 543162368 | bytes 6439936 | tf_op jit(solution)/shard_map/dot_general | solution.py:15
  39.2 0.0 copy-start.1
  39.2 1.9 %copy-done.1 = f32[256,4096]{1,0:T(8,128)} copy-done((f32[256,4096]{1,0:T(8,128)}, f32[256,4096]{1,0:T(8,128)S(1)}, u32[]{:S(2)}) %copy-start.1) | copy-done | bytes 4194328
  41.1 0.0 copy-done
  41.1 0.0 copy-start.3
  41.1 3.3 %convolution_bitcast_fusion = f32[16,256]{1,0:T(8,128)S(1)} fusion(f32[256,4096]{1,0:T(8,128)S(1)} %fusion.5, f32[16,4096]{1,0:T(8,128)S(1)} %copy-done), kind=kOutput, calls=%fused_computation.10 | convolution fusion | flops 201326592 | bytes 4472832 | tf_op jit(solution)/shard_map/dot_general | solution.py:35
  44.4 13.6 %all-gather = f32[128,256]{1,0:T(8,128)S(1)} all-gather(f32[16,256]{1,0:T(8,128)S(1)} %convolution_bitcast_fusion), channel_id=2, replica_groups=mesh['gx'=4,'gy'=8] {'gy'}, dimensions={0}, use_global_device_ids=true | all-gather | bytes 147456 | tf_op jit(solution)/shard_map/all_gather | solution.py:8
  58.1 20.4 %psum.14 = f32[16,256]{1,0:T(8,128)S(1)} all-reduce(f32[16,256]{1,0:T(8,128)S(1)} %reduce_sum.29), channel_id=1, replica_groups=mesh['gx'=4,'gy'=8] {'gx'}, use_global_device_ids=true, to_apply=%region_3.4 | all-reduce | flops 4096 | bytes 32768 | tf_op jit(solution)/shard_map/psum | solution.py:44
  78.5 0.0 copy-done.3
  78.5 29.9 %all_gather.15 = f32[16,256]{0,1:T(8,128)S(1)} all-gather(f32[16,8]{0,1:T(8,128)S(1)} %copy-done.3), channel_id=1, replica_groups=mesh['gx'=4,'gy'=8] {'gx','gy'}, dimensions={1}, use_global_device_ids=true | all-gather | bytes 16896 | tf_op jit(solution)/shard_map/all_gather | solution.py:45
  108.3 0.1 copy.13
  108.4 0.1 constant_dynamic-slice_fusion
  108.5 0.7 copy.15
  109.2 0.0 copy-start.5
  109.2 0.0 copy-start.2
  109.2 0.0 copy-start.4
  109.2 5.6 %copy.14 = f32[256,4096]{0,1:T(8,128)} copy(f32[256,4096]{1,0:T(8,128)} %copy-done.1) | data formatting | bytes 8388608 | tf_op jit(solution)/shard_map/exp | solution.py:17
  114.8 0.0 copy-done.5
  114.8 2.8 %gather_fusion.1 = f32[64,256]{1,0:T(8,128)S(1)} fusion(f32[256,4096]{0,1:T(8,128)} %copy.14, s32[1024]{0:T(1024)S(1)} %pad_clamp_fusion), kind=kCustom, calls=%fused_computation.1 | custom fusion | bytes 131328 | tf_op jit(solution)/shard_map/jit(_take)/gather | solution.py:38
  117.7 0.2 fusion.6
  117.9 0.0 copy-done.2
  117.9 0.1 convolution_bitcast_fusion.1
  118.1 48.8 %psum.15 = f32[128,16]{0,1:T(8,128)S(1)} all-reduce(f32[128,16]{0,1:T(8,128)S(1)} %convolution_bitcast_fusion.1), channel_id=1, replica_groups=mesh['gx'=4,'gy'=8] {'gx','gy'}, use_global_device_ids=true, to_apply=%region_4.5 | all-reduce | flops 2048 | bytes 16384 | tf_op jit(solution)/shard_map/psum | solution.py:21
  166.9 0.0 copy-done.4
  166.9 0.8 fusion.9
  (5 shorter events, 0.0 us)
Async XLA Ops:
  0.6 40.5 %copy-start = (f32[16,4096]{1,0:T(8,128)S(1)}, f32[16,4096]{1,0:T(8,128)}, u32[]{:S(2)}) copy-start(f32[16,4096]{1,0:T(8,128)} %param.8) | copy-start | bytes 786436
  39.2 1.9 %copy-start.1 = (f32[256,4096]{1,0:T(8,128)}, f32[256,4096]{1,0:T(8,128)S(1)}, u32[]{:S(2)}) copy-start(f32[256,4096]{1,0:T(8,128)S(1)} %fusion.5) | copy-start | bytes 12582916
  41.1 37.4 %copy-start.3 = (f32[16,8]{0,1:T(8,128)S(1)}, f32[16,8]{0,1:T(8,128)}, u32[]{:S(2)}) copy-start(f32[16,8]{0,1:T(8,128)} %param.9) | copy-start | bytes 1540
  109.2 5.6 %copy-start.5 = (s32[64]{0:T(128)S(1)}, s32[64]{0:T(128)}, u32[]{:S(2)}) copy-start(s32[64]{0:T(128)} %param.11) | copy-start | bytes 772
  109.2 8.7 %copy-start.2 = (f32[64,128]{1,0:T(8,128)S(1)}, f32[64,128]{1,0:T(8,128)}, u32[]{:S(2)}) copy-start(f32[64,128]{1,0:T(8,128)} %param.12) | copy-start | bytes 98308
  109.2 57.7 %copy-start.4 = (f32[128]{0:T(128)S(1)}, f32[128]{0:T(128)}, u32[]{:S(2)}) copy-start(f32[128]{0:T(128)} %param.13) | copy-start | bytes 1540
